TPU v7x, 32 devices: a whole 2x2x4 slice. The times are simulated.
32 devices in a mesh: dp: 4 (over y, x), expert: 8 (over z, core).
Axes of the slice: x: 2, y: 2, z: 4, core: 2. Of those that a mesh axis runs over, the one named last changes fastest.
Arguments:
- block_input: bfloat16 [6304, 768], P(('dp', 'expert')), may hold values from -12 to 12
- w_qkv: bfloat16 [768, 2304], P('dp'), may hold values from -0.21875 to 0.21875
- b_q: bfloat16 [768], P('dp'), may hold values from -3 to 3
- b_v: bfloat16 [768], P('dp'), may hold values from -3 to 3
- w_proj: bfloat16 [768, 768], P('dp'), may hold values from -1.75 to 1.75
- b_proj: bfloat16 [768], P('dp'), may hold values from -3 to 3
- ln1_gain: bfloat16 [768], P('dp'), may hold values from 0.099609375 to 1.8984375
- ln1_bias: bfloat16 [768], P('dp'), may hold values from -3 to 3
- ln2_gain: bfloat16 [768], P('dp'), may hold values from 0.099609375 to 1.8984375
- ln2_bias: bfloat16 [768], P('dp'), may hold values from -3 to 3
- w_router: bfloat16 [768, 8], P('dp'), may hold values from -0.4375 to 0.4375
- w_in: bfloat16 [8, 768, 3072], P('expert'), may hold values from -0.21875 to 0.21875
- b_in: bfloat16 [8, 3072], P('expert'), may hold values from -3 to 3
- w_out: bfloat16 [8, 3072, 768], P('expert'), may hold values from -0.109375 to 0.109375
- b_out: bfloat16 [8, 768], P('expert'), may hold values from -3 to 3
- routes: int32 [6304, 2], P(('dp', 'expert')), may hold values from 0 to 7, as said below
- slot_index: int32 [6304, 2], P(('dp', 'expert')), may hold values from 0 to 49, as said below
- d_out: bfloat16 [6304, 768], P(('dp', 'expert')), may hold values from -6 to 6
Outputs:
- block_out: bfloat16 [6304, 768], P(('dp', 'expert'))
- grad_input: float32 [6304, 768], P(('dp', 'expert'))
- d_w_qkv: float32 [768, 2304], P('dp')
- d_b_q: float32 [768], P('dp')
- d_b_v: float32 [768], P('dp')
- d_w_proj: float32 [768, 768], P('dp')
- d_b_proj: float32 [768], P('dp')
- d_ln1_gain: float32 [768], P('dp')
- d_ln1_bias: float32 [768], P('dp')
- d_ln2_gain: float32 [768], P('dp')
- d_ln2_bias: float32 [768], P('dp')
- d_w_router: float32 [768, 8], P('dp')
- d_w_in: float32 [8, 768, 3072], P('expert', 'dp')
- d_b_in: float32 [8, 3072], P('expert', 'dp')
- d_w_out: float32 [8, 3072, 768], P('expert', 'dp')
- d_b_out: float32 [8, 768], P('expert', 'dp')
Inputs may be any that keep to these rules, and one draw needn't show every extreme that they name: `routes`: each token names two different experts. slot_index[t, k] is the arrival position of choice k of token t at expert routes[t, k] among the tokens of one device, all first choices in token order before all second choices; 49 marks a choice that arrives beyond capacity and is dropped. In every draw one expert receives more than 49 first choices from every device.
All inputs are finite; a program needn't handle non-finite values.
Results may differ from a plain program's by a relative error of at most 0.012.
The roundings to bfloat16 on the way count: a program that leaves them out, or rounds other values in their place, can miss the bound.
Values may be sent and summed in bfloat16 or wider, within the bound.
No kernel may reach another device: no remote copies, remote signals or barrier semaphores. Data moves between devices by JAX's collectives and lax.ppermute only.
A program may use at most 128 MiB of HBM per device.

v0:
```python
import math
import jax
import jax.numpy as jnp
from jax import lax
from jax.sharding import PartitionSpec as P

HEAD_DIM = 64
SEQ = 197
NORM_EPS = 1e-06
SQRT_HALF = 0.7071067811865476
INV_ROOT_TWO_PI = 0.3989422804014327


def normalize(values):
    center = values - jnp.mean(values, axis=-1, keepdims=True)
    inv_std = lax.rsqrt(jnp.mean(center * center, axis=-1, keepdims=True) + NORM_EPS)
    return (center * inv_std, inv_std)


def norm_back(grad_in, normed, inv_std, gain_vec):
    scaled = grad_in * gain_vec
    mean_plain = jnp.mean(scaled, axis=-1, keepdims=True)
    mean_mixed = jnp.mean(scaled * normed, axis=-1, keepdims=True)
    return inv_std * (scaled - mean_plain - normed * mean_mixed)


def gelu_value(pre_act):
    return 0.5 * pre_act * (1.0 + lax.erf(pre_act * SQRT_HALF))


def gelu_slope(pre_act):
    return 0.5 * (1.0 + lax.erf(pre_act * SQRT_HALF)) + pre_act * INV_ROOT_TWO_PI * jnp.exp(
        -0.5 * pre_act * pre_act
    )


def by_heads(values, images):
    return values.reshape(images, SEQ, values.shape[1] // HEAD_DIM, HEAD_DIM)


def unpack(full_vectors):
    wide_vectors = full_vectors.astype(jnp.float32)
    return tuple((wide_vectors[index] for index in range(7)))


def slot_tables(routes, slot_table, experts, capacity):
    kept_mask = slot_table < capacity
    target = jnp.where(kept_mask, routes * capacity + slot_table, -1).reshape(-1)
    slot_match = target[:, None] == lax.broadcasted_iota(jnp.int32, (1, experts * capacity), 1)
    filled = jnp.any(slot_match, axis=0)
    choice_ids = lax.broadcasted_iota(jnp.int32, (target.shape[0], 1), 0)
    source = jnp.sum(jnp.where(slot_match, choice_ids, 0), axis=0, dtype=jnp.int32)
    return (kept_mask.reshape(-1), jnp.maximum(target, 0), filled, source)


def per_device(
    block_input,
    w_qkv,
    b_q,
    b_v,
    w_proj,
    b_proj,
    ln1_gain,
    ln1_bias,
    ln2_gain,
    ln2_bias,
    w_router,
    w_in,
    b_in,
    w_out,
    b_out,
    routes,
    slot_index,
    d_out,
):
    tokens = block_input.shape[0]
    width = block_input.shape[1]
    images = tokens // SEQ
    local_count = w_in.shape[0]
    hidden_units = w_in.shape[2]
    experts = local_count * lax.axis_size("expert")
    capacity = 2 * tokens // experts
    score_scale = 1.0 / math.sqrt(HEAD_DIM)
    vectors = jnp.stack([b_q, b_v, b_proj, ln1_gain, ln1_bias, ln2_gain, ln2_bias])
    full_qkv, full_proj, full_router, full_vectors = (
        lax.all_gather(w_qkv, "dp", axis=0, tiled=True),
        lax.all_gather(w_proj, "dp", axis=0, tiled=True),
        lax.all_gather(w_router, "dp", axis=0, tiled=True),
        lax.all_gather(vectors, "dp", axis=1, tiled=True),
    )
    bias_q, bias_v, bias_proj, gain_one, bias_one, gain_two, bias_two = unpack(full_vectors)
    resid = block_input.astype(jnp.float32)
    normed_one, inv_one = normalize(resid)
    a_in = (normed_one * gain_one + bias_one).astype(jnp.bfloat16)
    qkv = jnp.dot(a_in, full_qkv, preferred_element_type=jnp.float32)
    queries = (qkv[:, :width] + bias_q).astype(jnp.bfloat16)
    key_vecs = qkv[:, width : 2 * width].astype(jnp.bfloat16)
    values = (qkv[:, 2 * width :] + bias_v).astype(jnp.bfloat16)
    query_heads = by_heads(queries, images)
    key_heads = by_heads(key_vecs, images)
    value_heads = by_heads(values, images)
    scores = (
        jnp.einsum("bqhd,bkhd->bhqk", query_heads, key_heads, preferred_element_type=jnp.float32)
        * score_scale
    )
    row_max = jnp.max(scores, axis=-1, keepdims=True)
    exp_scores = jnp.exp(scores - row_max)
    row_total = jnp.sum(exp_scores, axis=-1, keepdims=True)
    log_total = row_max + jnp.log(row_total)
    probs_low = (exp_scores / row_total).astype(jnp.bfloat16)
    context = (
        jnp.einsum("bhqk,bkhd->bqhd", probs_low, value_heads, preferred_element_type=jnp.float32)
        .reshape(tokens, width)
        .astype(jnp.bfloat16)
    )
    hidden = resid + jnp.dot(context, full_proj, preferred_element_type=jnp.float32) + bias_proj
    normed_two, inv_two = normalize(hidden)
    y_in = (normed_two * gain_two + bias_two).astype(jnp.bfloat16)
    logits = jnp.dot(y_in, full_router, preferred_element_type=jnp.float32)
    route_hot = (routes[:, :, None] == lax.broadcasted_iota(jnp.int32, (1, 1, experts), 2)).astype(
        jnp.float32
    )
    chosen = jnp.sum(logits[:, None, :] * route_hot, axis=-1)
    first_gate = jax.nn.sigmoid(chosen[:, 0] - chosen[:, 1])
    gate_vals = jnp.stack([first_gate, 1.0 - first_gate], axis=1)
    kept_flat, fetch_index, filled, source = slot_tables(routes, slot_index, experts, capacity)
    sent_slots = jnp.where(filled[:, None], y_in[source // 2], 0).reshape(experts, capacity, width)
    bias_in = b_in.astype(jnp.float32)
    bias_out = b_out.astype(jnp.float32)
    received = lax.all_to_all(sent_slots, "expert", split_axis=0, concat_axis=0, tiled=True)
    slot_count = received.shape[1]
    grouped = received.reshape(-1, local_count, slot_count, width)
    pre_act = (
        jnp.einsum("necd,edf->necf", grouped, w_in, preferred_element_type=jnp.float32)
        + bias_in[None, :, None, :]
    )
    activated = gelu_value(pre_act).astype(jnp.bfloat16)
    down_proj = (
        jnp.einsum("necf,efd->necd", activated, w_out, preferred_element_type=jnp.float32)
        + bias_out[None, :, None, :]
    )
    received, pre_all, act_all, expert_out = (
        received,
        pre_act.reshape(-1, slot_count, hidden_units),
        activated.reshape(-1, slot_count, hidden_units),
        down_proj.astype(jnp.bfloat16).reshape(-1, slot_count, width),
    )
    returned = lax.all_to_all(expert_out, "expert", split_axis=0, concat_axis=0, tiled=True)
    picked = jnp.where(
        kept_flat[:, None],
        returned.reshape(experts * capacity, width)[fetch_index].astype(jnp.float32),
        0.0,
    ).reshape(tokens, 2, width)
    block_out = (hidden + jnp.sum(gate_vals[:, :, None] * picked, axis=1)).astype(jnp.bfloat16)
    grad_out = d_out.astype(jnp.float32)
    d_choice = (
        (gate_vals[:, :, None] * grad_out[:, None, :])
        .reshape(2 * tokens, width)
        .astype(jnp.bfloat16)
    )
    d_sent = jnp.where(filled[:, None], d_choice[source], 0).reshape(experts, capacity, width)
    d_gate = jnp.sum(grad_out[:, None, :] * picked, axis=-1)
    d_diff = (d_gate[:, 0] - d_gate[:, 1]) * gate_vals[:, 0] * gate_vals[:, 1]
    d_logits = (d_diff[:, None] * (route_hot[:, 0] - route_hot[:, 1])).astype(jnp.bfloat16)
    d_received = lax.all_to_all(d_sent, "expert", split_axis=0, concat_axis=0, tiled=True)
    grad_rows = d_received.reshape(-1, local_count, capacity, width)
    act_rows = act_all.reshape(-1, local_count, capacity, hidden_units)
    pre_rows = pre_all.reshape(-1, local_count, capacity, hidden_units)
    recv_rows = received.reshape(-1, local_count, capacity, width)
    d_b_out = jnp.sum(grad_rows.astype(jnp.float32), axis=(0, 2))
    d_w_out = jnp.einsum("necf,necd->efd", act_rows, grad_rows, preferred_element_type=jnp.float32)
    d_pre = jnp.einsum(
        "necd,efd->necf", grad_rows, w_out, preferred_element_type=jnp.float32
    ) * gelu_slope(pre_rows)
    d_b_in = jnp.sum(d_pre, axis=(0, 2))
    d_pre_low = d_pre.astype(jnp.bfloat16)
    d_w_in = jnp.einsum("necd,necf->edf", recv_rows, d_pre_low, preferred_element_type=jnp.float32)
    d_expert_in = (
        jnp.einsum("necf,edf->necd", d_pre_low, w_in, preferred_element_type=jnp.float32)
        .astype(jnp.bfloat16)
        .reshape(-1, capacity, width)
    )
    d_returned = lax.all_to_all(d_expert_in, "expert", split_axis=0, concat_axis=0, tiled=True)
    part_w_in, part_w_out, part_b_in, part_b_out = (
        lax.psum_scatter(d_w_in, "dp", scatter_dimension=1, tiled=True),
        lax.psum_scatter(d_w_out, "dp", scatter_dimension=1, tiled=True),
        lax.psum_scatter(d_b_in, "dp", scatter_dimension=1, tiled=True),
        lax.psum_scatter(d_b_out, "dp", scatter_dimension=1, tiled=True),
    )
    full_qkv, full_proj, full_router, full_vectors = (
        lax.all_gather(w_qkv, "dp", axis=0, tiled=True),
        lax.all_gather(w_proj, "dp", axis=0, tiled=True),
        lax.all_gather(w_router, "dp", axis=0, tiled=True),
        lax.all_gather(vectors, "dp", axis=1, tiled=True),
    )
    bias_q, bias_v, bias_proj, gain_one, bias_one, gain_two, bias_two = unpack(full_vectors)
    back_rows = jnp.where(
        kept_flat[:, None],
        d_returned.reshape(experts * capacity, width)[fetch_index].astype(jnp.float32),
        0.0,
    ).reshape(tokens, 2, width)
    d_w_router = jnp.einsum("td,te->de", y_in, d_logits, preferred_element_type=jnp.float32)
    d_y = jnp.sum(back_rows, axis=1) + jnp.einsum(
        "te,de->td", d_logits, full_router, preferred_element_type=jnp.float32
    )
    d_gain_two = jnp.sum(d_y * normed_two, axis=0)
    d_bias_two = jnp.sum(d_y, axis=0)
    d_hidden = grad_out + norm_back(d_y, normed_two, inv_two, gain_two)
    d_b_proj = jnp.sum(d_hidden, axis=0)
    d_hidden_low = d_hidden.astype(jnp.bfloat16)
    d_w_proj = jnp.einsum("td,te->de", context, d_hidden_low, preferred_element_type=jnp.float32)
    d_context = jnp.einsum(
        "te,de->td", d_hidden_low, full_proj, preferred_element_type=jnp.float32
    ).astype(jnp.bfloat16)
    grad_heads = by_heads(d_context, images)
    probs = jnp.exp(
        jnp.einsum("bqhd,bkhd->bhqk", query_heads, key_heads, preferred_element_type=jnp.float32)
        * score_scale
        - log_total
    )
    d_probs = jnp.einsum(
        "bqhd,bkhd->bhqk", grad_heads, value_heads, preferred_element_type=jnp.float32
    )
    d_values = jnp.einsum(
        "bhqk,bqhd->bkhd",
        probs.astype(jnp.bfloat16),
        grad_heads,
        preferred_element_type=jnp.float32,
    ).reshape(tokens, width)
    row_delta = jnp.sum(probs * d_probs, axis=-1, keepdims=True)
    d_scores = (probs * (d_probs - row_delta) * score_scale).astype(jnp.bfloat16)
    d_queries = jnp.einsum(
        "bhqk,bkhd->bqhd", d_scores, key_heads, preferred_element_type=jnp.float32
    ).reshape(tokens, width)
    d_keys = jnp.einsum(
        "bhqk,bqhd->bkhd", d_scores, query_heads, preferred_element_type=jnp.float32
    ).reshape(tokens, width)
    d_b_q = jnp.sum(d_queries, axis=0)
    d_b_v = jnp.sum(d_values, axis=0)
    d_qkv = jnp.concatenate([d_queries, d_keys, d_values], axis=1).astype(jnp.bfloat16)
    d_w_qkv = jnp.einsum("td,te->de", a_in, d_qkv, preferred_element_type=jnp.float32)
    d_a = jnp.einsum("te,de->td", d_qkv, full_qkv, preferred_element_type=jnp.float32)
    d_gain_one = jnp.sum(d_a * normed_one, axis=0)
    d_bias_one = jnp.sum(d_a, axis=0)
    d_input = d_hidden + norm_back(d_a, normed_one, inv_one, gain_one)
    grad_vectors = jnp.stack(
        [d_b_q, d_b_v, d_b_proj, d_gain_one, d_bias_one, d_gain_two, d_bias_two]
    )
    part_qkv, part_proj, part_router, part_vectors = (
        lax.psum_scatter(d_w_qkv, "dp", scatter_dimension=0, tiled=True),
        lax.psum_scatter(d_w_proj, "dp", scatter_dimension=0, tiled=True),
        lax.psum_scatter(d_w_router, "dp", scatter_dimension=0, tiled=True),
        lax.psum_scatter(grad_vectors, "dp", scatter_dimension=1, tiled=True),
    )
    sum_qkv, sum_proj, sum_router, sum_vectors = lax.psum(
        (part_qkv, part_proj, part_router, part_vectors), "expert"
    )
    return (
        block_out,
        d_input,
        sum_qkv,
        sum_vectors[0],
        sum_vectors[1],
        sum_proj,
        sum_vectors[2],
        sum_vectors[3],
        sum_vectors[4],
        sum_vectors[5],
        sum_vectors[6],
        sum_router,
        part_w_in,
        part_b_in,
        part_w_out,
        part_b_out,
    )


def solution(mesh):
    return jax.shard_map(
        per_device,
        mesh=mesh,
        in_specs=(
            P(("dp", "expert"), None),
            P("dp", None),
            P("dp"),
            P("dp"),
            P("dp", None),
            P("dp"),
            P("dp"),
            P("dp"),
            P("dp"),
            P("dp"),
            P("dp", None),
            P("expert", None, None),
            P("expert", None),
            P("expert", None, None),
            P("expert", None),
            P(("dp", "expert"), None),
            P(("dp", "expert"), None),
            P(("dp", "expert"), None),
        ),
        out_specs=(
            P(("dp", "expert"), None),
            P(("dp", "expert"), None),
            P("dp", None),
            P("dp"),
            P("dp"),
            P("dp", None),
            P("dp"),
            P("dp"),
            P("dp"),
            P("dp"),
            P("dp"),
            P("dp", None),
            P("expert", "dp", None),
            P("expert", "dp"),
            P("expert", "dp", None),
            P("expert", "dp"),
        ),
        check_vma=False,
    )
```

profile of v0, /device:TPU:0, one launch (start us, length us, event | category | flops | bytes accessed | tf_op | source)
XLA Modules:
  0.0 757.3 jit_solution(14147222516695071942)
XLA Ops:
  18.7 9.8 %all-gather = bf16[4,192,7]{1,2,0:T(8,128)(2,1)S(1)} all-gather(bf16[1,192,7]{1,2,0:T(8,128)(2,1)S(1)} %bitcast.203), channel_id=1, replica_groups=mesh['dp'=4,'expert'=8] {'dp'}, dimensions={0}, use_global_device_ids=true | all-gather | bytes 13440 | tf_op jit(solution)/shard_map/all_gather | solution.py:89
  29.9 30.1 %all-gather.5.cloned.1.call-done = bf16[768,2304]{1,0:T(8,128)(2,1)} async-done(((bf16[192,2304]{1,0:T(8,128)(2,1)}), bf16[768,2304]{1,0:T(8,128)(2,1)}) %all-gather.5.cloned.1.call-update) | async-done | bytes 3538960 | tf_op jit(solution)/shard_map/all_gather | solution.py:86
  69.3 20.2 %all-gather.7.cloned.1.call-done = bf16[768,768]{1,0:T(8,128)(2,1)} async-done(((bf16[192,768]{1,0:T(8,128)(2,1)}), bf16[768,768]{1,0:T(8,128)(2,1)}) %all-gather.7.cloned.1.call-update) | async-done | bytes 1179664 | tf_op jit(solution)/shard_map/all_gather | solution.py:87
  98.9 4.6 all-to-all-start
  103.5 18.8 %all-to-all-done = bf16[8,49,768]{2,1,0:T(8,128)(2,1)S(1)} async-done(((bf16[8,49,768]{2,1,0:T(8,128)(2,1)}), bf16[8,49,768]{2,1,0:T(8,128)(2,1)S(1)}, u32[]{:S(2)}, u32[]{:S(2)}) %all-to-all-start) | async-done | bytes 602144 | tf_op jit(solution)/shard_map/all_to_all | solution.py:130
  122.3 7.4 fusion.12
  129.7 7.1 fusion.44
  136.8 4.2 all-to-all-start.1
  141.1 8.6 %all-gather.1 = bf16[4,192,8]{1,2,0:T(8,128)(2,1)S(1)} all-gather(bf16[1,192,8]{1,2,0:T(8,128)(2,1)S(1)} %bitcast.211), channel_id=1, replica_groups=mesh['dp'=4,'expert'=8] {'dp'}, dimensions={0}, use_global_device_ids=true | all-gather | bytes 15360 | tf_op jit(solution)/shard_map/all_gather | solution.py:88
  155.4 4.5 all-to-all-done.1
  173.1 21.5 %all_to_all.20 = bf16[8,49,768]{2,1,0:T(8,128)(2,1)S(1)} all-to-all(bf16[8,49,768]{2,1,0:T(8,128)(2,1)S(1)} %broadcast_select_fusion), channel_id=1, replica_groups=mesh['dp'=4,'expert'=8] {'expert'}, dimensions={0} | all-to-all | bytes 1204224 | tf_op jit(solution)/shard_map/all_to_all | solution.py:165
  194.7 7.4 fusion.104
  203.6 3.3 fusion.36
  206.9 4.3 all-to-all-start.3
  213.3 16.8 %all-to-all-done.3 = bf16[8,49,768]{2,1,0:T(8,128)(2,1)} async-done(((bf16[8,49,768]{2,1,0:T(8,128)(2,1)}), bf16[8,49,768]{2,1,0:T(8,128)(2,1)}, u32[]{:S(2)}, u32[]{:S(2)}) %all-to-all-start.3) | async-done | bytes 602144 | tf_op jit(solution)/shard_map/all_to_all | solution.py:183
  236.9 7.8 %select_reduce_fusion = (f32[197,768]{1,0:T(8,128)S(1)}, f32[197,768]{1,0:T(8,128)S(1)}) fusion(f32[197,2,768]{2,1,0:T(2,128)} %reshape.385, pred[197,2]{1,0:T(8,128)(4,1)S(1)} %copy-done.27, f32[197,2,768]{2,1,0:T(2,128)} %reshape.384, f32[197,2]{1,0:T(8,128)S(1)} %copy.100), kind=kLoop, calls=%fused_computation.57 | loop fusion | flops 1210368 | bytes 3633074 | tf_op jit(solution)/shard_map/reduce_sum | solution.py:203
  253.8 3.0 fusion.106
  256.8 4.6 fusion.48
  261.5 4.8 fusion.98
  267.8 4.2 fusion.71
  276.8 3.5 fusion.67
  284.6 79.7 %reduce-scatter.17.cloned.1.call-done = f32[192,2304]{1,0:T(8,128)} async-done(((f32[768,2304]{1,0:T(8,128)}), f32[192,2304]{1,0:T(8,128)}) %reduce-scatter.17.cloned.1.call-update) | async-done | bytes 1769488 | tf_op jit(solution)/shard_map/reduce_scatter | solution.py:250
  364.4 6.9 convolution_bitcast_fusion
  372.3 7.0 convolution_bitcast_fusion.1
  379.3 12.0 %reduce-scatter.27.cloned.1.call-done = f32[192,8]{1,0:T(8,128)} async-done(((f32[768,8]{1,0:T(8,128)}), f32[192,8]{1,0:T(8,128)}) %reduce-scatter.27.cloned.1.call-update) | async-done | bytes 6160
  392.3 26.1 %reduce-scatter.31.cloned.1.call-done = f32[192,1]{1,0:T(8,128)} async-done(((f32[768,1]{1,0:T(8,128)}), f32[192,1]{1,0:T(8,128)}) %reduce-scatter.31.cloned.1.call-update) | async-done | bytes 784
  420.0 33.0 %reduce-scatter.29.cloned.1.call-done = f32[768,1]{1,0:T(8,128)} async-done(((f32[3072,1]{1,0:T(8,128)}), f32[768,1]{1,0:T(8,128)}) %reduce-scatter.29.cloned.1.call-update) | async-done | bytes 3088
  455.7 25.0 %reduce-scatter.25.cloned.1.call-done = f32[192,7]{1,0:T(8,128)} async-done(((f32[768,7]{1,0:T(8,128)}), f32[192,7]{1,0:T(8,128)}) %reduce-scatter.25.cloned.1.call-update) | async-done | bytes 5392
  481.7 29.6 %all-reduce = (f32[7,192]{1,0:T(8,128)S(1)}, f32[192,8]{0,1:T(8,128)}) all-reduce(f32[7,192]{1,0:T(8,128)S(1)} %copy.117, f32[192,8]{0,1:T(8,128)S(1)} %copy.119), channel_id=1, replica_groups=mesh['dp'=4,'expert'=8] {'expert'}, use_global_device_ids=true, to_apply=%region_27.28 | all-reduce | flops 2880 | bytes 23040 | tf_op jit(solution)/shard_map/psum | solution.py:255
  511.9 38.5 %all-reduce.4.cloned.1.call-done = (f32[192,2304]{1,0:T(8,128)}, f32[192,768]{1,0:T(8,128)}) async-done(((f32[192,2304]{1,0:T(8,128)}, f32[192,768]{1,0:T(8,128)}), (f32[192,2304]{1,0:T(8,128)}, f32[192,768]{1,0:T(8,128)})) %all-reduce.4.cloned.1.call-update) | async-done | bytes 2359312 | tf_op jit(solution)/shard_map/psum | solution.py:255
  550.4 97.7 %reduce-scatter.23.cloned.1.call-done = f32[1,768,768]{2,1,0:T(8,128)} async-done(((f32[1,3072,768]{2,1,0:T(8,128)}), f32[1,768,768]{2,1,0:T(8,128)}) %reduce-scatter.23.cloned.1.call-update) | async-done | bytes 2359312 | tf_op jit(solution)/shard_map/reduce_scatter | solution.py:186
  648.1 98.8 %reduce-scatter.21.cloned.1.call-done = f32[1,192,3072]{2,1,0:T(8,128)} async-done(((f32[1,768,3072]{2,1,0:T(8,128)}), f32[1,192,3072]{2,1,0:T(8,128)}) %reduce-scatter.21.cloned.1.call-update) | async-done | bytes 2359312 | tf_op jit(solution)/shard_map/reduce_scatter | solution.py:185
  (274 shorter events, 91.5 us)
Async XLA Ops:
  7.2 52.8 %copy-start.2 = (bf16[197,768]{1,0:T(8,128)(2,1)S(1)}, bf16[197,768]{1,0:T(8,128)(2,1)}, u32[]{:S(2)}) copy-start(bf16[197,768]{1,0:T(8,128)(2,1)} %param.18) | copy-start | bytes 907780
  7.2 52.8 %all-gather.5.cloned.1.call-start = ((), (), s32[]{:S(2)}) async-start(), calls=%async_computation.12 | async-start | bytes 4423680 | tf_op jit(solution)/shard_map/all_gather | solution.py:86
  7.9 81.6 %all-gather.7.cloned.1.call-start = ((), (), s32[]{:S(2)}) async-start(), calls=%async_computation.13 | async-start | bytes 1474560 | tf_op jit(solution)/shard_map/all_gather | solution.py:87
  11.7 51.3 %copy-start.42 = (f32[197]{0:T(256)}, f32[197]{0:T(256)S(1)}, u32[]{:S(2)}) copy-start(f32[197]{0:T(256)S(1)} %broadcast_multiply_fusion.5) | copy-start | bytes 2368
  12.9 50.0 %copy-start.46 = (f32[197]{0:T(256)}, f32[197]{0:T(256)S(1)}, u32[]{:S(2)}) copy-start(f32[197]{0:T(256)S(1)} %add_rsqrt_fusion.1) | copy-start | bytes 2368
  29.9 33.1 %copy-start.28 = (f32[768]{0:T(1024)}, f32[768]{0:T(1024)S(1)}, u32[]{:S(2)}) copy-start(f32[768]{0:T(1024)S(1)} %get-tuple-element.32) | copy-start | bytes 9220
  29.9 33.1 %copy-start.30 = (f32[768]{0:T(1024)}, f32[768]{0:T(1024)S(1)}, u32[]{:S(2)}) copy-start(f32[768]{0:T(1024)S(1)} %get-tuple-element.31) | copy-start | bytes 9220
  29.9 61.9 %copy-start.36 = (f32[768]{0:T(1024)}, f32[768]{0:T(1024)S(1)}, u32[]{:S(2)}) copy-start(f32[768]{0:T(1024)S(1)} %get-tuple-element.26) | copy-start | bytes 9220
  67.9 21.7 %copy-start.55 = (f32[768]{0:T(1024)S(1)}, f32[768]{0:T(1024)}, u32[]{:S(2)}) copy-start(f32[768]{0:T(1024)} %get-tuple-element.28) | copy-start | bytes 9220
  69.3 22.4 %copy-start.54 = (f32[768]{0:T(1024)S(1)}, f32[768]{0:T(1024)}, u32[]{:S(2)}) copy-start(f32[768]{0:T(1024)} %get-tuple-element.27) | copy-start | bytes 9220
  69.3 22.6 %copy-start.61 = (s32[1024]{0:T(1024)S(1)}, s32[1024]{0:T(1024)}, u32[]{:S(2)}) copy-start(s32[1024]{0:T(1024)} %pad_clamp_fusion.2) | copy-start | bytes 12292
  98.9 23.5 %all-to-all-start = ((bf16[8,49,768]{2,1,0:T(8,128)(2,1)}), bf16[8,49,768]{2,1,0:T(8,128)(2,1)S(1)}, u32[]{:S(2)}, u32[]{:S(2)}) async-start(bf16[8,49,768]{2,1,0:T(8,128)(2,1)} %broadcast_select_fusion.1), calls=%async_computation | async-start | bytes 1376256 | tf_op jit(solution)/shard_map/all_to_all | solution.py:130
  103.5 26.2 %copy-start.58 = (f32[1,3072]{1,0:T(1,128)}, f32[1,3072]{1,0:T(1,128)S(1)}, u32[]{:S(2)}) copy-start(f32[1,3072]{1,0:T(1,128)S(1)} %add.233) | copy-start | bytes 36868
  129.7 21.1 %copy-start.19 = (bf16[197,768]{1,0:T(8,128)(2,1)S(1)}, bf16[197,768]{1,0:T(8,128)(2,1)}, u32[]{:S(2)}) copy-start(bf16[197,768]{1,0:T(8,128)(2,1)} %param.35) | copy-start | bytes 907780
  136.8 23.1 %all-to-all-start.1 = ((bf16[8,49,768]{2,1,0:T(8,128)(2,1)}), bf16[8,49,768]{2,1,0:T(8,128)(2,1)}, u32[]{:S(2)}, u32[]{:S(2)}) async-start(bf16[8,49,768]{2,1,0:T(8,128)(2,1)} %fusion.44), calls=%async_computation.1 | async-start | bytes 1376256 | tf_op jit(solution)/shard_map/all_to_all | solution.py:148
  172.3 22.4 %copy-start.59 = (f32[1,3072]{1,0:T(1,128)S(1)}, f32[1,3072]{1,0:T(1,128)}, u32[]{:S(2)}) copy-start(f32[1,3072]{1,0:T(1,128)} %copy-done.58) | copy-start | bytes 36868
  173.1 30.5 %slice-start = ((s8[4718592]{0:T(1024)(128)(4,1)}), s8[4194304]{0:T(1024)(128)(4,1)S(1)}, s32[]{:S(2)}) async-start(s8[4718592]{0:T(1024)(128)(4,1)} %bitcast.180), calls=%async_computation.23 | async-start | bytes 8388608
  206.9 24.5 %copy-start.51 = (s32[1024]{0:T(1024)S(1)}, s32[1024]{0:T(1024)}, u32[]{:S(2)}) copy-start(s32[1024]{0:T(1024)} %copy-done.50) | copy-start | bytes 12292
  206.9 23.2 %all-to-all-start.3 = ((bf16[8,49,768]{2,1,0:T(8,128)(2,1)}), bf16[8,49,768]{2,1,0:T(8,128)(2,1)}, u32[]{:S(2)}, u32[]{:S(2)}) async-start(bf16[8,49,768]{2,1,0:T(8,128)(2,1)} %fusion.36), calls=%async_computation.3 | async-start | bytes 1376256 | tf_op jit(solution)/shard_map/all_to_all | solution.py:183
  211.2 73.3 %reduce-scatter.19.cloned.1.call-start = ((), (), s32[]{:S(2)}) async-start(), calls=%async_computation.15 | async-start | bytes 2949120 | tf_op jit(solution)/shard_map/reduce_scatter | solution.py:251
  213.3 31.5 %copy-start.40 = (bf16[197,8]{0,1:T(8,128)(2,1)}, bf16[197,8]{0,1:T(8,128)(2,1)S(1)}, u32[]{:S(2)}) copy-start(bf16[197,8]{0,1:T(8,128)(2,1)S(1)} %fusion.79) | copy-start | bytes 9460
  249.1 115.2 %reduce-scatter.17.cloned.1.call-start = ((), (), s32[]{:S(2)}) async-start(), calls=%async_computation.14 | async-start | bytes 8847360 | tf_op jit(solution)/shard_map/reduce_scatter | solution.py:250
  272.1 119.3 %reduce-scatter.27.cloned.1.call-start = ((), (), s32[]{:S(2)}) async-start(), calls=%async_computation.19 | async-start | bytes 491520
  273.8 144.6 %reduce-scatter.31.cloned.1.call-start = ((), (), s32[]{:S(2)}) async-start(), calls=%async_computation.21 | async-start | bytes 491520
  275.0 178.0 %reduce-scatter.29.cloned.1.call-start = ((), (), s32[]{:S(2)}) async-start(), calls=%async_computation.20 | async-start | bytes 1966080
  276.7 204.0 %reduce-scatter.25.cloned.1.call-start = ((), (), s32[]{:S(2)}) async-start(), calls=%async_computation.18 | async-start | bytes 491520
  280.3 84.0 %copy-start.60 = (f32[1,3072]{1,0:T(1,128)S(1)}, f32[1,3072]{1,0:T(1,128)}, u32[]{:S(2)}) copy-start(f32[1,3072]{1,0:T(1,128)} %copy-done.58) | copy-start | bytes 36868
  281.5 268.9 %all-reduce.4.cloned.1.call-start = ((), (), s32[]{:S(2)}) async-start(), calls=%async_computation.22 | async-start | bytes 4718592 | tf_op jit(solution)/shard_map/psum | solution.py:255
  364.3 283.8 %reduce-scatter.23.cloned.1.call-start = ((), (), s32[]{:S(2)}) async-start(), calls=%async_computation.17 | async-start | bytes 11796480 | tf_op jit(solution)/shard_map/reduce_scatter | solution.py:186
  371.3 375.6 %reduce-scatter.21.cloned.1.call-start = ((), (), s32[]{:S(2)}) async-start(), calls=%async_computation.16 | async-start | bytes 11796480 | tf_op jit(solution)/shard_map/reduce_scatter | solution.py:185
  379.3 75.4 %copy-start.6 = (f32[197,768]{1,0:T(8,128)S(1)}, f32[197,768]{1,0:T(8,128)}, u32[]{:S(2)}) copy-start(f32[197,768]{1,0:T(8,128)} %copy-done.4) | copy-start | bytes 1815556
  550.4 199.3 %copy-start.21 = (f32[192,768]{1,0:T(8,128)S(1)}, f32[192,768]{1,0:T(8,128)}, u32[]{:S(2)}) copy-start(f32[192,768]{1,0:T(8,128)} %get-tuple-element.80) | copy-start | bytes 1769476
  (53 other events, 285.6 us)
Sparse Core Ops, SparseCore 0:
  9.9 50.0 all-gather.4
  61.8 27.7 all-gather.6
  249.2 35.2 reduce-scatter.18
  287.5 76.7 reduce-scatter.16
  366.9 24.3 reduce-scatter.26
  394.0 24.4 reduce-scatter.30
  422.0 30.8 reduce-scatter.28
  456.3 24.4 reduce-scatter.24
  483.2 67.1 all-reduce.3
  554.0 94.1 reduce-scatter.22
  651.8 95.0 reduce-scatter.20
where the time goes:
time: 766 us; the launch traced here: 757 us
  waiting for transfers between devices  506 us (66%)
  matrix products  72.9 us (10%)
  blocking collectives  69.5 us (9%)
  local copies, waits for them, and re-layouts  57.3 us (7%)
  other arithmetic  22.9 us (3%)
  between operations  15 us (2%)
  starting transfers between devices  14 us (2%)
    reduce_scatter x1, waiting for transfers between devices, per_device(): lax.psum_scatter(d_w_in, 'dp', scatter_dimension=1, tiled=True)  98.8 us
    reduce_scatter x1, waiting for transfers between devices, per_device(): lax.psum_scatter(d_w_out, 'dp', scatter_dimension=1, tiled=True)  97.7 us
    unnamed x15, waiting for transfers between devices  97.6 us
    reduce_scatter x1, waiting for transfers between devices, per_device(): lax.psum_scatter(d_w_qkv, 'dp', scatter_dimension=0, tiled=True)  79.7 us
    psum x1, waiting for transfers between devices, per_device(): lax.psum((part_qkv, part_proj, part_router, part_vectors), 'expert')  38.5 us
    all_gather x1, waiting for transfers between devices, per_device(): lax.all_gather(w_qkv, 'dp', axis=0, tiled=True)  30.1 us
    psum x1, blocking collectives, per_device(): lax.psum((part_qkv, part_proj, part_router, part_vectors), 'expert')  29.6 us
    all_to_all x1, blocking collectives, per_device(): lax.all_to_all(d_sent, 'expert', split_axis=0, concat_axis=0, tiled=True)  21.5 us
  transfers between devices with their start and end apart: 14, of which 14 were waited for; matrix products, arithmetic and copies ran while one was open for 10% of the time, Pallas kernels for 0%

commit v1 on v0

--- a/solution.py
+++ b/solution.py
@@ -1,3 +1,4 @@
+import functools
 import math
 import jax
 import jax.numpy as jnp
@@ -9,6 +10,35 @@
 NORM_EPS = 1e-06
 SQRT_HALF = 0.7071067811865476
 INV_ROOT_TWO_PI = 0.3989422804014327
+
+
+def drive_groups(local_x, chip_axis, in_dim):
+    seen = []
+    dev_i = 0
+    dev_count = lax.axis_size(chip_axis)
+    while dev_i < dev_count:
+        seen.append((dev_i, (dev_i + 1) % dev_count))
+        dev_i = dev_i + 1
+    arrivals = []
+    dev_i = 0
+    while dev_i < dev_count:
+        arrivals.append((dev_i, (dev_i - 1) % dev_count))
+        dev_i = dev_i + 1
+    latest, p_next = ([local_x], [local_x])
+    for _ in range(dev_count // 2):
+        latest.append(lax.ppermute(latest[-1], chip_axis, seen))
+    b = 0
+    while b < (dev_count - 1) // 2:
+        p_next.append(lax.ppermute(p_next[-1], chip_axis, arrivals))
+        b = b + 1
+    return jnp.roll(
+        jnp.concatenate([*latest[::-1], *p_next[1:]], in_dim),
+        (lax.axis_index(chip_axis) - dev_count // 2) * local_x.shape[in_dim],
+        in_dim,
+    )
+
+
+_wrap_hubs = functools.partial(drive_groups, chip_axis="dp", in_dim=0)
 
 
 def normalize(values):
@@ -83,7 +113,7 @@
     score_scale = 1.0 / math.sqrt(HEAD_DIM)
     vectors = jnp.stack([b_q, b_v, b_proj, ln1_gain, ln1_bias, ln2_gain, ln2_bias])
     full_qkv, full_proj, full_router, full_vectors = (
-        lax.all_gather(w_qkv, "dp", axis=0, tiled=True),
+        _wrap_hubs(w_qkv),
         lax.all_gather(w_proj, "dp", axis=0, tiled=True),
         lax.all_gather(w_router, "dp", axis=0, tiled=True),
         lax.all_gather(vectors, "dp", axis=1, tiled=True),

time: 766 us -> 777 us (1.014)
  waiting for transfers between devices: 506 us -> 489 us
  blocking collectives: 69.5 us -> 82.8 us
  starting transfers between devices: 14 us -> 24.8 us
    all_gather x1, blocking collectives: 9.76 us -> 45.2 us  [per_device(): lax.all_gather(vectors, 'dp', axis=1, tiled=True)]
    all_gather x1, waiting for transfers between devices: 30.1 us -> 0.02 us  [per_device(): lax.all_gather(w_qkv, 'dp', axis=0, tiled=True)]
    all_to_all x1 -> x0, blocking collectives: 21.5 us -> none  [per_device(): lax.all_to_all(d_sent, 'expert', split_axis=0, concat_axis=0, tiled=True)]
    all_gather x1, waiting for transfers between devices: 20.2 us -> 0.01 us  [per_device(): lax.all_gather(w_proj, 'dp', axis=0, tiled=True)]
    all_to_all x0 -> x1, waiting for transfers between devices: none -> 18 us  [per_device(): lax.all_to_all(d_sent, 'expert', split_axis=0, concat_axis=0, tiled=True)]
    ppermute x0 -> x3, waiting for transfers between devices: none -> 15.3 us  [the longest x2 15.3 us: drive_groups(): latest.append(lax.ppermute(latest[-1], chip_axis, seen))]
    unnamed x154 -> x157, local copies, waits for them, and re-layouts: 19.4 us -> 21.5 us
  transfers between devices with their start and end apart: 14 -> 18, of which waited for: 14 -> 14; matrix products, arithmetic and copies ran while one was open for 10% -> 14% of each run, Pallas kernels for 0% -> 0%
where the time goes in v1:
time: 777 us; the launch traced here: 767 us
  waiting for transfers between devices  489 us (63%)
  blocking collectives  82.8 us (11%)
  matrix products  75 us (10%)
  local copies, waits for them, and re-layouts  57.8 us (7%)
  starting transfers between devices  24.8 us (3%)
  other arithmetic  23.2 us (3%)
  between operations  15.1 us (2%)
    reduce_scatter x1, waiting for transfers between devices, per_device(): lax.psum_scatter(d_w_out, 'dp', scatter_dimension=1, tiled=True)  98.8 us
    reduce_scatter x1, waiting for transfers between devices, per_device(): lax.psum_scatter(d_w_in, 'dp', scatter_dimension=1, tiled=True)  97.7 us
    unnamed x15, waiting for transfers between devices  97.4 us
    reduce_scatter x1, waiting for transfers between devices, per_device(): lax.psum_scatter(d_w_qkv, 'dp', scatter_dimension=0, tiled=True)  79.7 us
    all_gather x1, blocking collectives, per_device(): lax.all_gather(vectors, 'dp', axis=1, tiled=True)  45.2 us
    psum x1, waiting for transfers between devices, per_device(): lax.psum((part_qkv, part_proj, part_router, part_vectors), 'expert')  38.5 us
    psum x1, blocking collectives, per_device(): lax.psum((part_qkv, part_proj, part_router, part_vectors), 'expert')  29.6 us
    unnamed x157, local copies, waits for them, and re-layouts  21.5 us
  transfers between devices with their start and end apart: 18, of which 14 were waited for; matrix products, arithmetic and copies ran while one was open for 14% of the time, Pallas kernels for 0%

profile of v1, /device:TPU:0, one launch (start us, length us, event | category | flops | bytes accessed | tf_op | source)
XLA Modules:
  0.0 767.3 jit_solution(8529553946480580131)
XLA Ops:
  7.2 3.0 collective-permute-start
  15.9 45.2 %all-gather = bf16[4,192,7]{1,2,0:T(8,128)(2,1)S(1)} all-gather(bf16[1,192,7]{1,2,0:T(8,128)(2,1)S(1)} %bitcast.200), channel_id=1, replica_groups=mesh['dp'=4,'expert'=8] {'dp'}, dimensions={0}, use_global_device_ids=true | all-gather | bytes 13440 | tf_op jit(solution)/shard_map/all_gather | solution.py:119
  69.8 15.3 %collective-permute-done.1 = bf16[192,2304]{1,0:T(8,128)(2,1)S(1)} collective-permute-done((bf16[192,2304]{1,0:T(8,128)(2,1)S(1)}, bf16[192,2304]{1,0:T(8,128)(2,1)S(1)}, u32[]{:S(2)}, u32[]{:S(2)}) %collective-permute-start.1) | collective-permute-done | bytes 884768 | tf_op jit(solution)/shard_map/ppermute | solution.py:29
  103.6 4.9 all-to-all-start
  108.5 18.8 %all-to-all-done = bf16[8,49,768]{2,1,0:T(8,128)(2,1)S(1)} async-done(((bf16[8,49,768]{2,1,0:T(8,128)(2,1)}), bf16[8,49,768]{2,1,0:T(8,128)(2,1)S(1)}, u32[]{:S(2)}, u32[]{:S(2)}) %all-to-all-start) | async-done | bytes 602144 | tf_op jit(solution)/shard_map/all_to_all | solution.py:160
  127.3 7.3 fusion.12
  134.6 7.1 fusion.46
  141.7 4.8 all-to-all-start.1
  151.9 7.9 %all-gather.1 = bf16[4,192,8]{1,2,0:T(8,128)(2,1)S(1)} all-gather(bf16[1,192,8]{1,2,0:T(8,128)(2,1)S(1)} %bitcast.208), channel_id=1, replica_groups=mesh['dp'=4,'expert'=8] {'dp'}, dimensions={0}, use_global_device_ids=true | all-gather | bytes 15360 | tf_op jit(solution)/shard_map/all_gather | solution.py:118
  160.6 4.8 all-to-all-done.1
  179.4 3.5 all-to-all-start.2
  183.7 18.0 %all-to-all-done.2 = bf16[8,49,768]{2,1,0:T(8,128)(2,1)S(1)} async-done(((bf16[8,49,768]{2,1,0:T(8,128)(2,1)}), bf16[8,49,768]{2,1,0:T(8,128)(2,1)S(1)}, u32[]{:S(2)}, u32[]{:S(2)}) %all-to-all-start.2) | async-done | bytes 602144 | tf_op jit(solution)/shard_map/all_to_all | solution.py:195
  201.8 7.4 fusion.106
  210.8 6.3 fusion.38
  217.0 4.3 all-to-all-start.3
  223.4 16.8 %all-to-all-done.3 = bf16[8,49,768]{2,1,0:T(8,128)(2,1)} async-done(((bf16[8,49,768]{2,1,0:T(8,128)(2,1)}), bf16[8,49,768]{2,1,0:T(8,128)(2,1)}, u32[]{:S(2)}, u32[]{:S(2)}) %all-to-all-start.3) | async-done | bytes 602144 | tf_op jit(solution)/shard_map/all_to_all | solution.py:213
  247.1 7.8 %select_reduce_fusion = (f32[197,768]{1,0:T(8,128)S(1)}, f32[197,768]{1,0:T(8,128)S(1)}) fusion(f32[197,2,768]{2,1,0:T(2,128)} %reshape.385, pred[197,2]{1,0:T(8,128)(4,1)S(1)} %copy-done.29, f32[197,2,768]{2,1,0:T(2,128)} %reshape.384, f32[197,2]{1,0:T(8,128)S(1)} %copy.100), kind=kLoop, calls=%fused_computation.59 | loop fusion | flops 1210368 | bytes 3633074 | tf_op jit(solution)/shard_map/reduce_sum | solution.py:233
  267.1 4.7 fusion.50
  271.8 4.7 fusion.100
  278.0 4.2 fusion.73
  287.0 3.5 fusion.69
  294.6 79.7 %reduce-scatter.17.cloned.1.call-done = f32[192,2304]{1,0:T(8,128)} async-done(((f32[768,2304]{1,0:T(8,128)}), f32[192,2304]{1,0:T(8,128)}) %reduce-scatter.17.cloned.1.call-update) | async-done | bytes 1769488 | tf_op jit(solution)/shard_map/reduce_scatter | solution.py:280
  374.3 6.8 convolution_bitcast_fusion.1
  381.9 7.0 convolution_bitcast_fusion
  388.9 12.5 %reduce-scatter.27.cloned.1.call-done = f32[192,8]{1,0:T(8,128)} async-done(((f32[768,8]{1,0:T(8,128)}), f32[192,8]{1,0:T(8,128)}) %reduce-scatter.27.cloned.1.call-update) | async-done | bytes 6160
  402.3 26.1 %reduce-scatter.31.cloned.1.call-done = f32[192,1]{1,0:T(8,128)} async-done(((f32[768,1]{1,0:T(8,128)}), f32[192,1]{1,0:T(8,128)}) %reduce-scatter.31.cloned.1.call-update) | async-done | bytes 784
  430.0 33.0 %reduce-scatter.29.cloned.1.call-done = f32[768,1]{1,0:T(8,128)} async-done(((f32[3072,1]{1,0:T(8,128)}), f32[768,1]{1,0:T(8,128)}) %reduce-scatter.29.cloned.1.call-update) | async-done | bytes 3088
  465.8 25.0 %reduce-scatter.25.cloned.1.call-done = f32[192,7]{1,0:T(8,128)} async-done(((f32[768,7]{1,0:T(8,128)}), f32[192,7]{1,0:T(8,128)}) %reduce-scatter.25.cloned.1.call-update) | async-done | bytes 5392
  491.8 29.6 %all-reduce = (f32[7,192]{1,0:T(8,128)S(1)}, f32[192,8]{0,1:T(8,128)}) all-reduce(f32[7,192]{1,0:T(8,128)S(1)} %copy.117, f32[192,8]{0,1:T(8,128)S(1)} %copy.119), channel_id=1, replica_groups=mesh['dp'=4,'expert'=8] {'expert'}, use_global_device_ids=true, to_apply=%region_27.28 | all-reduce | flops 2880 | bytes 23040 | tf_op jit(solution)/shard_map/psum | solution.py:285
  521.9 38.5 %all-reduce.4.cloned.1.call-done = (f32[192,2304]{1,0:T(8,128)}, f32[192,768]{1,0:T(8,128)}) async-done(((f32[192,2304]{1,0:T(8,128)}, f32[192,768]{1,0:T(8,128)}), (f32[192,2304]{1,0:T(8,128)}, f32[192,768]{1,0:T(8,128)})) %all-reduce.4.cloned.1.call-update) | async-done | bytes 2359312 | tf_op jit(solution)/shard_map/psum | solution.py:285
  560.5 97.7 %reduce-scatter.21.cloned.1.call-done = f32[1,192,3072]{2,1,0:T(8,128)} async-done(((f32[1,768,3072]{2,1,0:T(8,128)}), f32[1,192,3072]{2,1,0:T(8,128)}) %reduce-scatter.21.cloned.1.call-update) | async-done | bytes 2359312 | tf_op jit(solution)/shard_map/reduce_scatter | solution.py:215
  658.2 98.8 %reduce-scatter.23.cloned.1.call-done = f32[1,768,768]{2,1,0:T(8,128)} async-done(((f32[1,3072,768]{2,1,0:T(8,128)}), f32[1,768,768]{2,1,0:T(8,128)}) %reduce-scatter.23.cloned.1.call-update) | async-done | bytes 2359312 | tf_op jit(solution)/shard_map/reduce_scatter | solution.py:216
  (284 shorter events, 97.0 us)
Async XLA Ops:
  7.2 78.1 %copy-start.7 = (bf16[192,2304]{1,0:T(8,128)(2,1)S(1)}, bf16[192,2304]{1,0:T(8,128)(2,1)}, u32[]{:S(2)}) copy-start(bf16[192,2304]{1,0:T(8,128)(2,1)} %param.19) | copy-start | bytes 2654212
  7.2 87.1 %all-gather.5.cloned.1.call-start = ((), (), s32[]{:S(2)}) async-start(), calls=%async_computation.12 | async-start | bytes 1474560 | tf_op jit(solution)/shard_map/all_gather | solution.py:117
  7.2 56.6 %collective-permute-start = (bf16[192,2304]{1,0:T(8,128)(2,1)}, bf16[192,2304]{1,0:T(8,128)(2,1)S(1)}, u32[]{:S(2)}, u32[]{:S(2)}) collective-permute-start(bf16[192,2304]{1,0:T(8,128)(2,1)} %param.19), channel_id=1, source_target_pairs={{0,8},{8,16},{16,24},{24,0},{1,9},{9,17},{17,25},{25,1},{2,10},{10... | collective-permute-start | bytes 2654216 | tf_op jit(solution)/shard_map/ppermute | solution.py:29
  10.2 75.1 %collective-permute-start.2 = (bf16[192,2304]{1,0:T(8,128)(2,1)}, bf16[192,2304]{1,0:T(8,128)(2,1)S(1)}, u32[]{:S(2)}, u32[]{:S(2)}) collective-permute-start(bf16[192,2304]{1,0:T(8,128)(2,1)} %param.19), channel_id=1, source_target_pairs={{0,24},{8,0},{16,8},{24,16},{1,25},{9,1},{17,9},{25,17},{2,26},{10... | collective-permute-start | bytes 2654216 | tf_op jit(solution)/shard_map/ppermute | solution.py:32
  63.9 21.5 %copy-start.11 = (bf16[192,2304]{1,0:T(8,128)(2,1)}, bf16[192,2304]{1,0:T(8,128)(2,1)S(1)}, u32[]{:S(2)}) copy-start(bf16[192,2304]{1,0:T(8,128)(2,1)S(1)} %collective-permute-done) | copy-start | bytes 2654212
  63.9 21.2 %collective-permute-start.1 = (bf16[192,2304]{1,0:T(8,128)(2,1)S(1)}, bf16[192,2304]{1,0:T(8,128)(2,1)S(1)}, u32[]{:S(2)}, u32[]{:S(2)}) collective-permute-start(bf16[192,2304]{1,0:T(8,128)(2,1)S(1)} %collective-permute-done), channel_id=1, source_target_pairs={{0,8},{8,16},{16,24},{24,0},{1,9},{9,17},{17,25},{25,1},{2,10},{10... | collective-permute-start | bytes 2654216 | tf_op jit(solution)/shard_map/ppermute | solution.py:29
  67.5 19.2 %copy-start.30 = (f32[768]{0:T(1024)}, f32[768]{0:T(1024)S(1)}, u32[]{:S(2)}) copy-start(f32[768]{0:T(1024)S(1)} %get-tuple-element.32) | copy-start | bytes 9220
  67.5 19.3 %copy-start.32 = (f32[768]{0:T(1024)}, f32[768]{0:T(1024)S(1)}, u32[]{:S(2)}) copy-start(f32[768]{0:T(1024)S(1)} %get-tuple-element.31) | copy-start | bytes 9220
  67.5 29.0 %copy-start.38 = (f32[768]{0:T(1024)}, f32[768]{0:T(1024)S(1)}, u32[]{:S(2)}) copy-start(f32[768]{0:T(1024)S(1)} %get-tuple-element.26) | copy-start | bytes 9220
  68.6 18.2 %copy-start.44 = (f32[197]{0:T(256)}, f32[197]{0:T(256)S(1)}, u32[]{:S(2)}) copy-start(f32[197]{0:T(256)S(1)} %broadcast_multiply_fusion.5) | copy-start | bytes 2368
  69.8 16.9 %copy-start.48 = (f32[197]{0:T(256)}, f32[197]{0:T(256)S(1)}, u32[]{:S(2)}) copy-start(f32[197]{0:T(256)S(1)} %add_rsqrt_fusion.1) | copy-start | bytes 2368
  103.6 23.7 %all-to-all-start = ((bf16[8,49,768]{2,1,0:T(8,128)(2,1)}), bf16[8,49,768]{2,1,0:T(8,128)(2,1)S(1)}, u32[]{:S(2)}, u32[]{:S(2)}) async-start(bf16[8,49,768]{2,1,0:T(8,128)(2,1)} %broadcast_select_fusion.1), calls=%async_computation | async-start | bytes 1376256 | tf_op jit(solution)/shard_map/all_to_all | solution.py:160
  108.5 26.1 %copy-start.59 = (f32[1,3072]{1,0:T(1,128)}, f32[1,3072]{1,0:T(1,128)S(1)}, u32[]{:S(2)}) copy-start(f32[1,3072]{1,0:T(1,128)S(1)} %add.246) | copy-start | bytes 36868
  141.7 23.7 %all-to-all-start.1 = ((bf16[8,49,768]{2,1,0:T(8,128)(2,1)}), bf16[8,49,768]{2,1,0:T(8,128)(2,1)}, u32[]{:S(2)}, u32[]{:S(2)}) async-start(bf16[8,49,768]{2,1,0:T(8,128)(2,1)} %fusion.46), calls=%async_computation.1 | async-start | bytes 1376256 | tf_op jit(solution)/shard_map/all_to_all | solution.py:178
  146.5 13.6 %copy-start.50 = (s32[197,2]{0,1:T(2,128)S(1)}, s32[197,2]{0,1:T(2,128)}, u32[]{:S(2)}) copy-start(s32[197,2]{0,1:T(2,128)} %param.33) | copy-start | bytes 4732
  179.4 22.3 %all-to-all-start.2 = ((bf16[8,49,768]{2,1,0:T(8,128)(2,1)}), bf16[8,49,768]{2,1,0:T(8,128)(2,1)S(1)}, u32[]{:S(2)}, u32[]{:S(2)}) async-start(bf16[8,49,768]{2,1,0:T(8,128)(2,1)} %broadcast_select_fusion), calls=%async_computation.2 | async-start | bytes 1376256 | tf_op jit(solution)/shard_map/all_to_all | solution.py:195
  183.0 104.0 %all-gather.7.cloned.1.call-start = ((), (), s32[]{:S(2)}) async-start(), calls=%async_computation.13 | async-start | bytes 4423680 | tf_op jit(solution)/shard_map/all_gather | solution.py:221
  217.0 24.5 %copy-start.53 = (s32[1024]{0:T(1024)S(1)}, s32[1024]{0:T(1024)}, u32[]{:S(2)}) copy-start(s32[1024]{0:T(1024)} %copy-done.52) | copy-start | bytes 12292
  217.0 23.2 %all-to-all-start.3 = ((bf16[8,49,768]{2,1,0:T(8,128)(2,1)}), bf16[8,49,768]{2,1,0:T(8,128)(2,1)}, u32[]{:S(2)}, u32[]{:S(2)}) async-start(bf16[8,49,768]{2,1,0:T(8,128)(2,1)} %fusion.38), calls=%async_computation.3 | async-start | bytes 1376256 | tf_op jit(solution)/shard_map/all_to_all | solution.py:213
  221.4 73.2 %reduce-scatter.19.cloned.1.call-start = ((), (), s32[]{:S(2)}) async-start(), calls=%async_computation.15 | async-start | bytes 2949120 | tf_op jit(solution)/shard_map/reduce_scatter | solution.py:281
  223.4 31.5 %copy-start.42 = (bf16[197,8]{0,1:T(8,128)(2,1)}, bf16[197,8]{0,1:T(8,128)(2,1)S(1)}, u32[]{:S(2)}) copy-start(bf16[197,8]{0,1:T(8,128)(2,1)S(1)} %fusion.81) | copy-start | bytes 9460
  259.3 114.9 %reduce-scatter.17.cloned.1.call-start = ((), (), s32[]{:S(2)}) async-start(), calls=%async_computation.14 | async-start | bytes 8847360 | tf_op jit(solution)/shard_map/reduce_scatter | solution.py:280
  282.3 119.1 %reduce-scatter.27.cloned.1.call-start = ((), (), s32[]{:S(2)}) async-start(), calls=%async_computation.19 | async-start | bytes 491520
  284.0 144.4 %reduce-scatter.31.cloned.1.call-start = ((), (), s32[]{:S(2)}) async-start(), calls=%async_computation.21 | async-start | bytes 491520
  285.2 177.8 %reduce-scatter.29.cloned.1.call-start = ((), (), s32[]{:S(2)}) async-start(), calls=%async_computation.20 | async-start | bytes 1966080
  286.9 203.8 %reduce-scatter.25.cloned.1.call-start = ((), (), s32[]{:S(2)}) async-start(), calls=%async_computation.18 | async-start | bytes 491520
  290.6 83.7 %copy-start.9 = (bf16[8,49,768]{2,1,0:T(8,128)(2,1)S(1)}, bf16[8,49,768]{2,1,0:T(8,128)(2,1)}, u32[]{:S(2)}) copy-start(bf16[8,49,768]{2,1,0:T(8,128)(2,1)} %copy-done.8) | copy-start | bytes 1806340
  291.8 268.6 %all-reduce.4.cloned.1.call-start = ((), (), s32[]{:S(2)}) async-start(), calls=%async_computation.22 | async-start | bytes 4718592 | tf_op jit(solution)/shard_map/psum | solution.py:285
  374.3 283.9 %reduce-scatter.21.cloned.1.call-start = ((), (), s32[]{:S(2)}) async-start(), calls=%async_computation.16 | async-start | bytes 11796480 | tf_op jit(solution)/shard_map/reduce_scatter | solution.py:215
  381.2 375.7 %reduce-scatter.23.cloned.1.call-start = ((), (), s32[]{:S(2)}) async-start(), calls=%async_computation.17 | async-start | bytes 11796480 | tf_op jit(solution)/shard_map/reduce_scatter | solution.py:216
  388.9 75.8 %copy-start.6 = (f32[197,768]{1,0:T(8,128)S(1)}, f32[197,768]{1,0:T(8,128)}, u32[]{:S(2)}) copy-start(f32[197,768]{1,0:T(8,128)} %copy-done.4) | copy-start | bytes 1815556
  560.5 199.3 %copy-start.23 = (f32[192,768]{1,0:T(8,128)S(1)}, f32[192,768]{1,0:T(8,128)}, u32[]{:S(2)}) copy-start(f32[192,768]{1,0:T(8,128)} %get-tuple-element.80) | copy-start | bytes 1769476
  (55 other events, 248.9 us)
Sparse Core Ops, SparseCore 0:
  11.4 42.9 all-gather.4
  185.7 47.4 all-gather.6
  259.4 35.0 reduce-scatter.18
  297.5 76.7 reduce-scatter.16
  376.9 24.4 reduce-scatter.26
  404.0 24.4 reduce-scatter.30
  432.0 30.9 reduce-scatter.28
  466.3 24.4 reduce-scatter.24
  493.2 67.1 all-reduce.3
  564.0 94.1 reduce-scatter.20
  661.9 95.0 reduce-scatter.22
